TPU v7x, 512 devices: a whole 4x4x16 slice. The times are simulated.
512 devices in a mesh: slab: 64 (over z, x_hi, core), band: 8 (over y, x_lo).
Axes of the slice: x: 4 (x_hi: 2, x_lo: 2; x = x_hi * 2 + x_lo), y: 4, z: 16, core: 2. Of those that a mesh axis runs over, the one named last changes fastest.
Arguments:
- hamiltonian: bfloat16 [512, 7, 128, 128], P('slab', None, 'band'), may hold values from -0.1875 to 0.1875
- neighbors: int32 [512, 7], P('slab'), may hold values from 0 to 11, as said below
- orbitals: bfloat16 [65536, 1024], P('slab', 'band'), may hold values from -6 to 6
Outputs:
- residual: bfloat16 [65536, 1024], P(('slab', 'band'))
Inputs may be any that keep to these rules, and one draw needn't show every extreme that they name: `neighbors`: window positions 0 to 1 are the last 2 elements of the slab below (periodic), 2 to 9 the slab's own elements, the rest the first 2 elements of the slab above. A slab's elements are in layers of 2; each block row names, in an order of its own, itself, the element 2 positions below and above it in the window, and four elements of its own layer (repeats possible).
All inputs are finite; a program needn't handle non-finite values.
Results may differ from a plain program's by a relative error of at most 0.012.
Values may be sent and summed in bfloat16 or wider, within the bound.
No kernel may reach another device: no remote copies, remote signals or barrier semaphores. Data moves between devices by JAX's collectives and lax.ppermute only.
A program may use at most 64 MiB of HBM per device.

v0:
```python
import math
import jax
import jax.numpy as jnp
from jax import lax
from jax.sharding import PartitionSpec as P

FACE = 2


def padded(block, sides, width):
    for axis, dim in sides:
        count = lax.axis_size(axis)
        forward = [(i, i + 1) for i in range(count - 1)]
        forward.append((count - 1, 0))
        backward = [(target, source) for source, target in forward]
        low = lax.ppermute(
            lax.slice_in_dim(block, block.shape[dim] - width, None, axis=dim), axis, forward
        )
        high = lax.ppermute(lax.slice_in_dim(block, 0, width, axis=dim), axis, backward)
        block = jnp.concatenate([low, block, high], axis=dim)
    return block


def apply_local(vector, full_tiles, neighbors):
    tile_size = full_tiles.shape[2]
    extended = padded(vector, (("slab", 0),), FACE * tile_size)
    blocks = extended.reshape(-1, tile_size, vector.shape[1])
    picked_blocks = blocks[neighbors]
    product = jnp.einsum(
        "rjab,rjbc->rac", full_tiles, picked_blocks, preferred_element_type=jnp.float32
    )
    return product.reshape(vector.shape[0], vector.shape[1])


def body(hamiltonian, neighbors, orbitals):
    full_tiles = lax.all_gather(hamiltonian, "band", axis=2, tiled=True)
    first = apply_local(orbitals, full_tiles, neighbors).astype(jnp.bfloat16)
    second = (
        2.0 * apply_local(first, full_tiles, neighbors) - orbitals.astype(jnp.float32)
    ).astype(jnp.bfloat16)
    third = (2.0 * apply_local(second, full_tiles, neighbors) - first.astype(jnp.float32)).astype(
        jnp.bfloat16
    )
    applied = apply_local(third, full_tiles, neighbors).astype(jnp.bfloat16)
    rows_all = orbitals.shape[0] * lax.axis_size("slab")
    bands_all = orbitals.shape[1] * lax.axis_size("band")
    gram_scale = 1.0 / math.sqrt(float(rows_all) * float(bands_all))
    strip_third, strip_applied = (
        lax.all_to_all(third, "band", split_axis=0, concat_axis=1, tiled=True),
        lax.all_to_all(applied, "band", split_axis=0, concat_axis=1, tiled=True),
    )
    partial_value = jnp.einsum(
        "rb,rc->bc", strip_third, strip_applied, preferred_element_type=jnp.float32
    )
    summed = lax.psum(partial_value, ("slab", "band"))
    gram_full = (summed * gram_scale).astype(jnp.bfloat16)
    mixed = jnp.dot(strip_third, gram_full, preferred_element_type=jnp.float32)
    return (strip_applied.astype(jnp.float32) - mixed).astype(jnp.bfloat16)


def solution(mesh):
    in_specs = (P("slab", None, "band", None), P("slab", None), P("slab", "band"))
    out_specs = P(("slab", "band"), None)
    return jax.shard_map(body, mesh=mesh, in_specs=in_specs, out_specs=out_specs, check_vma=False)
```

profile of v0, /device:TPU:2, one launch (start us, length us, event | category | flops | bytes accessed | tf_op | source)
XLA Modules:
  0.0 640.3 jit_solution(16940214057220224389)
XLA Ops:
  6.5 0.0 all-gather.2.cloned.1.call-start
  6.5 0.7 all-gather.2.cloned.1.call-update
  7.3 0.9 fusion.16
  8.1 1.9 collective-permute-start
  10.1 12.4 %collective-permute-start.1 = (bf16[256,128]{1,0:T(8,128)(2,1)S(1)}, bf16[256,128]{1,0:T(8,128)(2,1)S(1)}, u32[]{:S(2)}, u32[]{:S(2)}) collective-permute-start(bf16[256,128]{1,0:T(8,128)(2,1)S(1)} %get-tuple-element.12), channel_id=1, source_target_pairs={{8,0},{16,8},{24,16},{32,24},{40,32},{48,40},{56,48},{64,56},{72,6... | collective-permute-start | bytes 196616 | tf_op jit(solution)/shard_map/ppermute | solution.py:19
  22.5 0.7 compare_select_fusion
  23.2 0.1 reshape.35
  23.3 0.0 collective-permute-done
  23.3 1.1 collective-permute-done.1
  24.4 1.0 pad_maximum_fusion
  25.3 0.9 gather_fusion
  26.3 42.6 %all-gather.2.cloned.1.call-done = bf16[8,7,128,128]{3,2,1,0:T(8,128)(2,1)} async-done(((bf16[8,7,16,128]{3,2,1,0:T(8,128)(2,1)}), bf16[8,7,128,128]{3,2,1,0:T(8,128)(2,1)}) %all-gather.2.cloned.1.call-update) | async-done | bytes 1835024 | tf_op jit(solution)/shard_map/all_gather | solution.py:36
  68.9 2.1 fusion.6
  71.0 3.2 collective-permute-start.3
  74.2 1.9 collective-permute-start.2
  76.2 0.0 collective-permute-done.3
  76.2 7.3 %collective-permute-done.2 = bf16[256,128]{1,0:T(8,128)(2,1)S(1)} collective-permute-done((bf16[256,128]{1,0:T(8,128)(2,1)S(1)}, bf16[256,128]{1,0:T(8,128)(2,1)S(1)}, u32[]{:S(2)}, u32[]{:S(2)}) %collective-permute-start.2) | collective-permute-done | bytes 65568 | tf_op jit(solution)/shard_map/ppermute | solution.py:16
  83.5 0.0 copy-start
  83.5 2.0 gather_fusion.1
  85.5 0.0 copy-done
  85.5 0.0 copy-start.1
  85.5 2.2 fusion.3
  87.7 0.0 copy-done.1
  87.7 0.1 fusion.10
  87.8 1.9 collective-permute-start.4
  89.7 7.3 %collective-permute-start.5 = (bf16[256,128]{1,0:T(8,128)(2,1)S(1)}, bf16[256,128]{1,0:T(8,128)(2,1)S(1)}, u32[]{:S(2)}, u32[]{:S(2)}) collective-permute-start(bf16[256,128]{1,0:T(8,128)(2,1)S(1)} %get-tuple-element.8), channel_id=1, source_target_pairs={{8,0},{16,8},{24,16},{32,24},{40,32},{48,40},{56,48},{64,56},{72,6... | collective-permute-start | bytes 196616 | tf_op jit(solution)/shard_map/ppermute | solution.py:19
  97.0 0.0 collective-permute-done.4
  97.0 1.9 collective-permute-done.5
  98.9 2.1 gather_fusion.2
  101.0 2.1 fusion.4
  103.1 0.1 fusion.9
  103.2 1.9 collective-permute-start.6
  105.1 7.3 %collective-permute-start.7 = (bf16[256,128]{1,0:T(8,128)(2,1)S(1)}, bf16[256,128]{1,0:T(8,128)(2,1)S(1)}, u32[]{:S(2)}, u32[]{:S(2)}) collective-permute-start(bf16[256,128]{1,0:T(8,128)(2,1)S(1)} %get-tuple-element.6), channel_id=1, source_target_pairs={{8,0},{16,8},{24,16},{32,24},{40,32},{48,40},{56,48},{64,56},{72,6... | collective-permute-start | bytes 196616 | tf_op jit(solution)/shard_map/ppermute | solution.py:19
  112.4 0.8 fusion.11
  113.2 6.0 all-to-all-start.1
  119.2 0.0 collective-permute-done.6
  119.2 0.0 collective-permute-done.7
  119.3 2.1 gather_fusion.3
  121.4 3.0 fusion.8
  124.3 1.0 all-to-all-done.1
  125.4 4.7 all-to-all-start
  130.0 0.0 all-reduce.2.cloned.1.call-start
  130.0 0.2 copy.7
  130.2 5.9 all-to-all-done
  136.2 2.7 fusion.17
  138.9 0.0 all-reduce.2.cloned.1.call-update
  138.9 0.1 copy.6
  139.0 491.1 %all-reduce.2.cloned.1.call-done = f32[1024,1024]{1,0:T(8,128)} async-done(((f32[1024,1024]{1,0:T(8,128)}), f32[1024,1024]{1,0:T(8,128)}) %all-reduce.2.cloned.1.call-update) | async-done | bytes 4194320 | tf_op jit(solution)/shard_map/psum | solution.py:55
  630.1 3.4 fusion.7
  (7 shorter events, 0.1 us)
Async XLA Ops:
  6.5 62.3 %all-gather.2.cloned.1.call-start = ((), (), s32[]{:S(2)}) async-start(), calls=%async_computation.2 | async-start | bytes 2064384 | tf_op jit(solution)/shard_map/all_gather | solution.py:36
  8.1 15.1 %collective-permute-start = (bf16[256,128]{1,0:T(8,128)(2,1)S(1)}, bf16[256,128]{1,0:T(8,128)(2,1)S(1)}, u32[]{:S(2)}, u32[]{:S(2)}) collective-permute-start(bf16[256,128]{1,0:T(8,128)(2,1)S(1)} %get-tuple-element.11), channel_id=1, source_target_pairs={{0,8},{8,16},{16,24},{24,32},{32,40},{40,48},{48,56},{56,64},{64,7... | collective-permute-start | bytes 196616 | tf_op jit(solution)/shard_map/ppermute | solution.py:16
  10.1 14.3 %collective-permute-start.1 = (bf16[256,128]{1,0:T(8,128)(2,1)S(1)}, bf16[256,128]{1,0:T(8,128)(2,1)S(1)}, u32[]{:S(2)}, u32[]{:S(2)}) collective-permute-start(bf16[256,128]{1,0:T(8,128)(2,1)S(1)} %get-tuple-element.12), channel_id=1, source_target_pairs={{8,0},{16,8},{24,16},{32,24},{40,32},{48,40},{56,48},{64,56},{72,6... | collective-permute-start | bytes 196616 | tf_op jit(solution)/shard_map/ppermute | solution.py:19
  71.0 5.2 collective-permute-start.3
  74.2 9.2 %collective-permute-start.2 = (bf16[256,128]{1,0:T(8,128)(2,1)S(1)}, bf16[256,128]{1,0:T(8,128)(2,1)S(1)}, u32[]{:S(2)}, u32[]{:S(2)}) collective-permute-start(bf16[256,128]{1,0:T(8,128)(2,1)S(1)} %bitcast.83), channel_id=1, source_target_pairs={{0,8},{8,16},{16,24},{24,32},{32,40},{40,48},{48,56},{56,64},{64,7... | collective-permute-start | bytes 196616 | tf_op jit(solution)/shard_map/ppermute | solution.py:16
  83.5 2.0 copy-start
  85.5 2.2 copy-start.1
  87.8 9.2 %collective-permute-start.4 = (bf16[256,128]{1,0:T(8,128)(2,1)S(1)}, bf16[256,128]{1,0:T(8,128)(2,1)S(1)}, u32[]{:S(2)}, u32[]{:S(2)}) collective-permute-start(bf16[256,128]{1,0:T(8,128)(2,1)S(1)} %get-tuple-element.7), channel_id=1, source_target_pairs={{0,8},{8,16},{16,24},{24,32},{32,40},{40,48},{48,56},{56,64},{64,7... | collective-permute-start | bytes 196616 | tf_op jit(solution)/shard_map/ppermute | solution.py:16
  89.7 9.1 %collective-permute-start.5 = (bf16[256,128]{1,0:T(8,128)(2,1)S(1)}, bf16[256,128]{1,0:T(8,128)(2,1)S(1)}, u32[]{:S(2)}, u32[]{:S(2)}) collective-permute-start(bf16[256,128]{1,0:T(8,128)(2,1)S(1)} %get-tuple-element.8), channel_id=1, source_target_pairs={{8,0},{16,8},{24,16},{32,24},{40,32},{48,40},{56,48},{64,56},{72,6... | collective-permute-start | bytes 196616 | tf_op jit(solution)/shard_map/ppermute | solution.py:19
  103.2 16.1 %collective-permute-start.6 = (bf16[256,128]{1,0:T(8,128)(2,1)S(1)}, bf16[256,128]{1,0:T(8,128)(2,1)S(1)}, u32[]{:S(2)}, u32[]{:S(2)}) collective-permute-start(bf16[256,128]{1,0:T(8,128)(2,1)S(1)} %get-tuple-element.5), channel_id=1, source_target_pairs={{0,8},{8,16},{16,24},{24,32},{32,40},{40,48},{48,56},{56,64},{64,7... | collective-permute-start | bytes 196616 | tf_op jit(solution)/shard_map/ppermute | solution.py:16
  105.1 14.1 %collective-permute-start.7 = (bf16[256,128]{1,0:T(8,128)(2,1)S(1)}, bf16[256,128]{1,0:T(8,128)(2,1)S(1)}, u32[]{:S(2)}, u32[]{:S(2)}) collective-permute-start(bf16[256,128]{1,0:T(8,128)(2,1)S(1)} %get-tuple-element.6), channel_id=1, source_target_pairs={{8,0},{16,8},{24,16},{32,24},{40,32},{48,40},{56,48},{64,56},{72,6... | collective-permute-start | bytes 196616 | tf_op jit(solution)/shard_map/ppermute | solution.py:19
  113.2 12.2 %all-to-all-start.1 = ((bf16[8,128,128]{2,1,0:T(8,128)(2,1)}), bf16[8,128,128]{2,1,0:T(8,128)(2,1)S(1)}, u32[]{:S(2)}, u32[]{:S(2)}) async-start(bf16[8,128,128]{2,1,0:T(8,128)(2,1)} %fusion.11), calls=%async_computation.1 | async-start | bytes 524288 | tf_op jit(solution)/shard_map/all_to_all | solution.py:49
  125.4 10.8 %all-to-all-start = ((bf16[8,128,128]{1,2,0:T(8,128)(2,1)}), bf16[8,128,128]{1,2,0:T(8,128)(2,1)S(1)}, u32[]{:S(2)}, u32[]{:S(2)}) async-start(bf16[8,128,128]{1,2,0:T(8,128)(2,1)} %fusion.8), calls=%async_computation | async-start | bytes 524288 | tf_op jit(solution)/shard_map/all_to_all | solution.py:50
  130.0 500.1 %all-reduce.2.cloned.1.call-start = ((), (), s32[]{:S(2)}) async-start(), calls=%async_computation.3 | async-start | bytes 8388608 | tf_op jit(solution)/shard_map/psum | solution.py:55
Sparse Core Ops, SparseCore 0:
  9.3 59.4 all-gather.1
  139.0 491.0 all-reduce.1
where the time goes:
time: 641 us; the launch traced here: 640 us
  waiting for transfers between devices  552 us (86%)
  starting transfers between devices  48.6 us (8%)
  matrix products  15.5 us (2%)
  between operations  13.6 us (2%)
  local copies, waits for them, and re-layouts  8.39 us (1%)
    psum x1, waiting for transfers between devices, body(): summed = lax.psum(partial_value, ('slab', 'band'))  491 us
    all_gather x1, waiting for transfers between devices, body(): full_tiles = lax.all_gather(hamiltonian, 'band', axis=2, tiled=True)  42.6 us
    ppermute x4, starting transfers between devices, padded(): lax.ppermute(lax.slice_in_dim(block, 0, width, axis=dim), axis, backward)  30.2 us
  transfers between devices with their start and end apart: 12, of which 7 were waited for; matrix products, arithmetic and copies ran while one was open for 2% of the time, Pallas kernels for 0%

commit v1 on v0

--- a/solution.py
+++ b/solution.py
@@ -52,7 +52,7 @@
     partial_value = jnp.einsum(
         "rb,rc->bc", strip_third, strip_applied, preferred_element_type=jnp.float32
     )
-    summed = lax.psum(partial_value, ("slab", "band"))
+    summed = lax.psum(lax.psum(partial_value, "slab"), "band")
     gram_full = (summed * gram_scale).astype(jnp.bfloat16)
     mixed = jnp.dot(strip_third, gram_full, preferred_element_type=jnp.float32)
     return (strip_applied.astype(jnp.float32) - mixed).astype(jnp.bfloat16)

time: 641 us -> 890 us (1.39)
  the two profiles are of different devices: /device:TPU:2 before, /device:TPU:1 now
where the time goes in v1:
time: 890 us; the launch traced here: 889 us
  waiting for transfers between devices  804 us (90%)
  starting transfers between devices  45.5 us (5%)
  matrix products  15.5 us (2%)
  between operations  13.3 us (1%)
    psum x2, waiting for transfers between devices, body(): summed = lax.psum(lax.psum(partial_value, 'slab'), 'band')  746 us
    all_gather x1, waiting for transfers between devices, body(): full_tiles = lax.all_gather(hamiltonian, 'band', axis=2, tiled=True)  44.6 us
    ppermute x4, starting transfers between devices, padded(): lax.ppermute(lax.slice_in_dim(block, 0, width, axis=dim), axis, backward)  18.9 us
    ppermute x4, starting transfers between devices, padded(): lax.ppermute(lax.slice_in_dim(block, block.shape[dim] - width, None, axis...  18.2 us
  transfers between devices with their start and end apart: 13, of which 8 were waited for; matrix products, arithmetic and copies ran while one was open for 1% of the time, Pallas kernels for 0%

profile of v1, /device:TPU:1, one launch (start us, length us, event | category | flops | bytes accessed | tf_op | source)
XLA Modules:
  0.0 889.3 jit_solution(10123520747897578629)
XLA Ops:
  6.5 0.0 all-gather.2.cloned.1.call-start
  6.5 0.7 all-gather.2.cloned.1.call-update
  7.3 0.9 fusion.16
  8.1 6.0 collective-permute-start
  14.2 4.6 collective-permute-start.1
  18.8 0.7 compare_select_fusion
  19.5 0.1 reshape.35
  19.6 0.0 collective-permute-done
  19.6 1.7 collective-permute-done.1
  21.3 1.0 pad_maximum_fusion
  22.3 0.9 gather_fusion
  23.2 44.6 %all-gather.2.cloned.1.call-done = bf16[8,7,128,128]{3,2,1,0:T(8,128)(2,1)} async-done(((bf16[8,7,16,128]{3,2,1,0:T(8,128)(2,1)}), bf16[8,7,128,128]{3,2,1,0:T(8,128)(2,1)}) %all-gather.2.cloned.1.call-update) | async-done | bytes 1835024 | tf_op jit(solution)/shard_map/all_gather | solution.py:36
  67.7 2.1 fusion.6
  69.9 4.5 collective-permute-start.3
  74.4 4.4 collective-permute-start.2
  78.8 0.0 collective-permute-done.3
  78.8 1.3 collective-permute-done.2
  80.2 0.0 copy-start
  80.2 2.0 gather_fusion.1
  82.2 0.0 copy-done
  82.2 0.0 copy-start.1
  82.2 2.2 fusion.3
  84.4 0.0 copy-done.1
  84.4 0.1 fusion.10
  84.5 5.8 collective-permute-start.4
  90.3 3.9 collective-permute-start.5
  94.1 0.0 collective-permute-done.4
  94.1 3.2 collective-permute-done.5
  97.4 2.1 gather_fusion.2
  99.4 2.1 fusion.4
  101.6 0.1 fusion.9
  101.7 1.9 collective-permute-start.6
  103.6 5.9 collective-permute-start.7
  109.5 0.8 fusion.11
  110.3 4.2 all-to-all-start.1
  114.5 0.0 collective-permute-done.6
  114.5 0.0 collective-permute-done.7
  114.6 2.1 gather_fusion.3
  116.6 3.0 fusion.8
  119.6 1.0 all-to-all-done.1
  120.7 4.1 all-to-all-start
  124.8 0.0 all-reduce.3.cloned.1.call-start
  124.8 0.2 copy.7
  125.0 5.9 all-to-all-done
  130.9 2.7 fusion.17
  133.6 0.0 all-reduce.3.cloned.1.call-update
  133.6 0.0 all-reduce.5.cloned.1.call-start
  133.7 546.1 %all-reduce.3.cloned.1.call-done = f32[1024,1024]{1,0:T(8,128)} async-done(((f32[1024,1024]{1,0:T(8,128)}), f32[1024,1024]{1,0:T(8,128)}) %all-reduce.3.cloned.1.call-update) | async-done | bytes 4194320 | tf_op jit(solution)/shard_map/psum | solution.py:55
  679.8 0.0 all-reduce.5.cloned.1.call-update
  679.8 0.1 copy.6
  680.0 199.4 %all-reduce.5.cloned.1.call-done = f32[1024,1024]{1,0:T(8,128)} async-done(((f32[1024,1024]{1,0:T(8,128)}), f32[1024,1024]{1,0:T(8,128)}) %all-reduce.5.cloned.1.call-update) | async-done | bytes 4194320 | tf_op jit(solution)/shard_map/psum | solution.py:55
  879.4 3.4 fusion.7
  (7 shorter events, 0.1 us)
Async XLA Ops:
  6.5 61.2 %all-gather.2.cloned.1.call-start = ((), (), s32[]{:S(2)}) async-start(), calls=%async_computation.2 | async-start | bytes 2064384 | tf_op jit(solution)/shard_map/all_gather | solution.py:36
  8.1 11.5 %collective-permute-start = (bf16[256,128]{1,0:T(8,128)(2,1)S(1)}, bf16[256,128]{1,0:T(8,128)(2,1)S(1)}, u32[]{:S(2)}, u32[]{:S(2)}) collective-permute-start(bf16[256,128]{1,0:T(8,128)(2,1)S(1)} %get-tuple-element.11), channel_id=1, source_target_pairs={{0,8},{8,16},{16,24},{24,32},{32,40},{40,48},{48,56},{56,64},{64,7... | collective-permute-start | bytes 196616 | tf_op jit(solution)/shard_map/ppermute | solution.py:16
  14.2 7.1 collective-permute-start.1
  69.9 8.9 %collective-permute-start.3 = (bf16[256,128]{1,0:T(8,128)(2,1)S(1)}, bf16[256,128]{1,0:T(8,128)(2,1)S(1)}, u32[]{:S(2)}, u32[]{:S(2)}) collective-permute-start(bf16[256,128]{1,0:T(8,128)(2,1)S(1)} %bitcast.84), channel_id=1, source_target_pairs={{8,0},{16,8},{24,16},{32,24},{40,32},{48,40},{56,48},{64,56},{72,6... | collective-permute-start | bytes 196616 | tf_op jit(solution)/shard_map/ppermute | solution.py:19
  74.4 5.8 collective-permute-start.2
  80.2 2.0 copy-start
  82.2 2.2 copy-start.1
  84.5 9.7 %collective-permute-start.4 = (bf16[256,128]{1,0:T(8,128)(2,1)S(1)}, bf16[256,128]{1,0:T(8,128)(2,1)S(1)}, u32[]{:S(2)}, u32[]{:S(2)}) collective-permute-start(bf16[256,128]{1,0:T(8,128)(2,1)S(1)} %get-tuple-element.7), channel_id=1, source_target_pairs={{0,8},{8,16},{16,24},{24,32},{32,40},{40,48},{48,56},{56,64},{64,7... | collective-permute-start | bytes 196616 | tf_op jit(solution)/shard_map/ppermute | solution.py:16
  90.3 7.1 collective-permute-start.5
  101.7 12.9 %collective-permute-start.6 = (bf16[256,128]{1,0:T(8,128)(2,1)S(1)}, bf16[256,128]{1,0:T(8,128)(2,1)S(1)}, u32[]{:S(2)}, u32[]{:S(2)}) collective-permute-start(bf16[256,128]{1,0:T(8,128)(2,1)S(1)} %get-tuple-element.5), channel_id=1, source_target_pairs={{0,8},{8,16},{16,24},{24,32},{32,40},{40,48},{48,56},{56,64},{64,7... | collective-permute-start | bytes 196616 | tf_op jit(solution)/shard_map/ppermute | solution.py:16
  103.6 10.9 %collective-permute-start.7 = (bf16[256,128]{1,0:T(8,128)(2,1)S(1)}, bf16[256,128]{1,0:T(8,128)(2,1)S(1)}, u32[]{:S(2)}, u32[]{:S(2)}) collective-permute-start(bf16[256,128]{1,0:T(8,128)(2,1)S(1)} %get-tuple-element.6), channel_id=1, source_target_pairs={{8,0},{16,8},{24,16},{32,24},{40,32},{48,40},{56,48},{64,56},{72,6... | collective-permute-start | bytes 196616 | tf_op jit(solution)/shard_map/ppermute | solution.py:19
  110.3 10.3 %all-to-all-start.1 = ((bf16[8,128,128]{2,1,0:T(8,128)(2,1)}), bf16[8,128,128]{2,1,0:T(8,128)(2,1)S(1)}, u32[]{:S(2)}, u32[]{:S(2)}) async-start(bf16[8,128,128]{2,1,0:T(8,128)(2,1)} %fusion.11), calls=%async_computation.1 | async-start | bytes 524288 | tf_op jit(solution)/shard_map/all_to_all | solution.py:49
  120.7 10.2 %all-to-all-start = ((bf16[8,128,128]{1,2,0:T(8,128)(2,1)}), bf16[8,128,128]{1,2,0:T(8,128)(2,1)S(1)}, u32[]{:S(2)}, u32[]{:S(2)}) async-start(bf16[8,128,128]{1,2,0:T(8,128)(2,1)} %fusion.8), calls=%async_computation | async-start | bytes 524288 | tf_op jit(solution)/shard_map/all_to_all | solution.py:50
  124.8 555.0 %all-reduce.3.cloned.1.call-start = ((), (), s32[]{:S(2)}) async-start(), calls=%async_computation.3 | async-start | bytes 8388608 | tf_op jit(solution)/shard_map/psum | solution.py:55
  133.6 745.8 %all-reduce.5.cloned.1.call-start = ((), (), s32[]{:S(2)}) async-start(), calls=%async_computation.4 | async-start | bytes 8388608 | tf_op jit(solution)/shard_map/psum | solution.py:55
Sparse Core Ops, SparseCore 0:
  9.3 58.3 all-gather.1
  133.7 546.0 all-reduce.2
  682.8 196.5 all-reduce.4
